TPU v7x, 128 devices: a whole 4x4x4 slice. The times are simulated.
128 devices in a mesh: row: 8 (over z_hi, y), col: 16 (over x, z_lo, core).
Axes of the slice: x: 4, y: 4, z: 4 (z_hi: 2, z_lo: 2; z = z_hi * 2 + z_lo), core: 2. Of those that a mesh axis runs over, the one named last changes fastest.
Arguments:
- vectors: bfloat16 [32, 524288], P(None, ('row', 'col')), may hold values from -6 to 6
- tile_values: bfloat16 [81920, 128, 128], P(('row', 'col')), may hold values from -0.0546875 to 0.0546875
- tile_rows: int32 [81920], P(('row', 'col')), may hold values from 0 to 511
- tile_cols: int32 [81920], P(('row', 'col')), may hold values from 0 to 255
- tile_count: int32 [128], P(('row', 'col')), may hold values from 160 to 640, as said below
Outputs:
- filtered: bfloat16 [32, 524288], P(None, ('row', 'col'))
Inputs may be any that keep to these rules, and one draw needn't show every extreme that they name: `tile_count`: every device has at least a quarter of its slots live and some device has all 640 live.
All inputs are finite; a program needn't handle non-finite values.
Results may differ from a plain program's by a relative error of at most 0.014.
Values may be sent and summed in bfloat16 or wider, within the bound.
A program may use at most 128 MiB of HBM per device.

v0:
```python
import jax
import jax.numpy as jnp
from jax import lax
from jax.experimental import pallas as pl
from jax.experimental.pallas import tpu as pltpu
from jax.sharding import PartitionSpec as P

MESH = pl.DeviceIdType.MESH
VMEM = pltpu.VMEM
HALF = 16
CHUNK = 32
UNROLL = 16
RING = 8


def place():
    row, col = lax.axis_index("row"), lax.axis_index("col")
    return row % 4, row // 4, col // 4, (col // 2) % 2, col % 2


def col_of(x, zl, core):
    return lax.rem(x, 4) * 4 + zl * 2 + core


def row_of(y, zh):
    return zh * 4 + lax.rem(y, 4)


class Net:
    def __init__(self):
        self.y, self.zh, self.x, self.zl, self.core = y, zh, x, zl, core = place()
        row, col = lax.axis_index("row"), lax.axis_index("col")
        self.row, self.col = row, col
        self.right = (row, col_of(x + 1, zl, core))
        self.left = (row, col_of(x + 3, zl, core))
        self.zpair = (row, col_of(x, 1 - zl, core))
        self.mate = (row, col_of(x, zl, 1 - core))
        self.up = (row_of(y + 1, zh), col)
        self.down = (row_of(y + 3, zh), col)
        self.zfar = (row_of(y, 1 - zh), col)

    def own_col(self, dx, p):
        return col_of(self.x + dx, self.zl if p == 0 else 1 - self.zl, self.core)

    def mate_col(self, dx, p):
        return col_of(self.x + dx, self.zl if p == 0 else 1 - self.zl, 1 - self.core)

    def own_row(self, dy, q):
        return row_of(self.y + dy, self.zh if q == 0 else 1 - self.zh)

    def barrier(self):
        sem = pltpu.get_barrier_semaphore()
        peers = (self.right, self.left, self.zpair, self.mate, self.up, self.down, self.zfar)
        for peer in peers:
            pl.semaphore_signal(sem, inc=1, device_id=peer, device_id_type=MESH)
        pl.semaphore_wait(sem, len(peers))


class Sends:
    def __init__(self, sems):
        self.sems, self.copies = sems, []

    def __call__(self, src, dst, recv, peer):
        copy = pltpu.make_async_remote_copy(
            src_ref=src,
            dst_ref=dst,
            send_sem=self.sems.at[len(self.copies)],
            recv_sem=recv,
            device_id=peer,
            device_id_type=MESH,
        )
        copy.start()
        self.copies.append(copy)

    def drain(self):
        for copy in self.copies:
            copy.wait_send()


def await_copy(ref, sem):
    pltpu.make_async_copy(ref, ref, sem).wait()


def half(h):
    return pl.ds(HALF * h, HALF)


GATHER_SENDS = 44


def gather_kernel(v, xr, xc, keep, send_sems, z_in, x_in, fx_in, m_in, zf_in, y_in, fy_in):
    net = Net()
    send = Sends(send_sems)

    def r_at(dx, p, h):
        return xr.at[net.own_col(dx, p), half(h)]

    def m_at(dx, p, h):
        return xr.at[net.mate_col(dx, p), half(h)]

    def c_at(dy, q, h):
        return xc.at[net.own_row(dy, q), half(h)]

    own = [
        pltpu.make_async_copy(v, xr.at[net.col], keep.at[0]),
        pltpu.make_async_copy(v, xc.at[net.row], keep.at[1]),
    ]
    net.barrier()
    for h in range(2):
        send(v.at[half(h)], c_at(0, 0, h), zf_in.at[h], net.zfar)
    for i in range(2):
        for h, way, x_peer, y_peer in ((i, 0, net.right, net.up), (1 - i, 1, net.left, net.down)):
            send(v.at[half(h)], r_at(0, 0, h), x_in.at[way, 0, h], x_peer)
            send(v.at[half(h)], c_at(0, 0, h), y_in.at[way, 0, h], y_peer)
    for h in range(2):
        send(v.at[half(h)], r_at(0, 0, h), z_in.at[0, h], net.zpair)
    for h in range(2):
        send(v.at[half(h)], r_at(0, 0, h), m_in.at[0, 0, h], net.mate)
    for copy in own:
        copy.start()

    def pass_on(dx, p, h, sem, peer):
        send(r_at(dx, p, h), r_at(dx, p, h), sem, peer)

    def pass_up(dy, q, h, sem, peer):
        send(c_at(dy, q, h), c_at(dy, q, h), sem, peer)

    def to_mate(dx, p, h):
        pass_on(dx, p, h, m_in.at[dx, p, h], net.mate)

    def x_came(way, p, h):
        dx = 3 if way == 0 else 1
        await_copy(r_at(dx, p, h), x_in.at[way, p, h])
        if p == 0 and h == way:
            pass_on(dx, 0, h, fx_in.at[way], net.right if way == 0 else net.left)
        to_mate(dx, p, h)

    def y_came(way, q, h):
        dy = 3 if way == 0 else 1
        await_copy(c_at(dy, q, h), y_in.at[way, q, h])
        if h == way:
            pass_up(dy, q, h, fy_in.at[way, q], net.up if way == 0 else net.down)

    for way in range(2):
        x_came(way, 0, way)
        y_came(way, 0, way)
    for way in range(2):
        x_came(way, 0, 1 - way)
        y_came(way, 0, 1 - way)
    await_copy(c_at(0, 1, 0), zf_in.at[0])
    pass_up(0, 1, 0, y_in.at[0, 1, 0], net.up)
    await_copy(c_at(0, 1, 1), zf_in.at[1])
    pass_up(0, 1, 1, y_in.at[1, 1, 1], net.down)
    pass_up(0, 1, 1, y_in.at[0, 1, 1], net.up)
    pass_up(0, 1, 0, y_in.at[1, 1, 0], net.down)
    for h in range(2):
        await_copy(r_at(0, 1, h), z_in.at[0, h])
        pass_on(0, 1, h, x_in.at[0, 1, h], net.right)
        pass_on(0, 1, h, x_in.at[1, 1, h], net.left)
        to_mate(0, 1, h)
        await_copy(r_at(2, 0, h), fx_in.at[h])
        pass_on(2, 0, h, z_in.at[1, h], net.zpair)
        to_mate(2, 0, h)
    for way in range(2):
        y_came(way, 1, way)
    for h in range(2):
        for way in range(2):
            x_came(way, 1, h)
    for h in range(2):
        await_copy(r_at(2, 1, h), z_in.at[1, h])
        to_mate(2, 1, h)
    for way in range(2):
        await_copy(c_at(2, 0, way), fy_in.at[way, 0])
        y_came(way, 1, 1 - way)
    for h in range(2):
        await_copy(c_at(2, 1, h), fy_in.at[h, 1])
    for dx in (0, 3, 1, 2):
        for p in range(2):
            for h in range(2):
                await_copy(m_at(dx, p, h), m_in.at[dx, p, h])
    for copy in own:
        copy.wait()
    send.drain()
    assert len(send.copies) == GATHER_SENDS


def gather(v):
    k, n = v.shape
    dma = pltpu.SemaphoreType.DMA
    return pl.pallas_call(
        gather_kernel,
        out_shape=[jax.ShapeDtypeStruct((16, k, n), v.dtype), jax.ShapeDtypeStruct((8, k, n), v.dtype)],
        in_specs=[pl.BlockSpec(memory_space=VMEM)],
        out_specs=[pl.BlockSpec(memory_space=pl.ANY)] * 2,
        scratch_shapes=[
            dma((2,)),
            dma((GATHER_SENDS,)),
            dma((2, 2)),
            dma((2, 2, 2)),
            dma((2,)),
            dma((4, 2, 2)),
            dma((2,)),
            dma((2, 2, 2)),
            dma((2, 2)),
        ],
        compiler_params=pltpu.CompilerParams(collective_id=0, has_side_effects=True, vmem_limit_bytes=4 << 20),
        name="panels",
    )(v)


def product_kernel(count, rows, cols, xr, xc, tiles_hbm, out_r, out_c, tiles, acc_r, acc_c, sems):
    live = count[0]
    chunks = (live + CHUNK - 1) // CHUNK

    def fetch(i):
        n = lax.rem(i, RING)
        return pltpu.make_async_copy(tiles_hbm.at[pl.ds(i * CHUNK, CHUNK)], tiles.at[n], sems.at[n])

    @pl.loop(0, jnp.minimum(chunks, RING))
    def _(i):
        fetch(i).start()

    @pl.loop(0, 16)
    def _(i):
        acc_r[i] = jnp.zeros(acc_r.shape[1:], jnp.float32)

    @pl.loop(0, 8)
    def _(i):
        acc_c[i] = jnp.zeros(acc_c.shape[1:], jnp.float32)

    def lanes(block):
        return pl.ds(pl.multiple_of(lax.rem(block, 32) * 128, 128), 128)

    none = jnp.zeros((32, 128), jnp.bfloat16)

    def both(x, y):
        return jnp.concatenate([jnp.concatenate([x, none], axis=1), jnp.concatenate([none, y], axis=1)], axis=0)

    @pl.loop(0, chunks)
    def _(i):
        fetch(i).wait()
        n = lax.rem(i, RING)

        @pl.loop(0, CHUNK // UNROLL)
        def _(j):
            found = []
            for u in range(0, UNROLL, 2):
                at = j * UNROLL + u
                s = i * CHUNK + at
                rb, cb = [rows[s], rows[s + 1]], [cols[s], cols[s + 1]]
                t = tiles[n, pl.ds(at, 2)]
                x_c = both(*[xc[b // 32, :, lanes(b)] for b in cb])
                x_r = both(*[xr[b // 32, :, lanes(b)] for b in rb])
                wide = jnp.concatenate([t[0], t[1]], axis=1)
                to_r = lax.dot_general(x_c, wide, (((1,), (1,)), ((), ())), preferred_element_type=jnp.float32)
                tall = t.reshape(256, 128)
                to_c = lax.dot_general(x_r, tall, (((1,), (0,)), ((), ())), preferred_element_type=jnp.float32)
                for e in range(2):
                    part = slice(32 * e, 32 * e + 32)
                    found.append((rb[e], cb[e], s + e < live, to_r[part], to_c[part]))
            for rb, cb, ok, to_r, to_c in found:
                rd = jnp.where(ok, rb // 32, 16)
                cd = jnp.where(ok, cb // 32, 8)
                acc_r[rd, :, lanes(rb)] += to_r
                acc_c[cd, :, lanes(cb)] += to_c

        @pl.when(i + RING < chunks)
        def _():
            fetch(i + RING).start()

    @pl.loop(0, 16)
    def _(i):
        out_r[i] = acc_r[i].astype(jnp.bfloat16)

    @pl.loop(0, 8)
    def _(i):
        out_c[i] = acc_c[i].astype(jnp.bfloat16)


def products(count, rows, cols, xr, xc, tiles):
    k, n = xr.shape[1:]
    smem = pl.BlockSpec(memory_space=pltpu.SMEM)
    vmem = pl.BlockSpec(memory_space=VMEM)
    return pl.pallas_call(
        product_kernel,
        out_shape=[jax.ShapeDtypeStruct(xr.shape, xr.dtype), jax.ShapeDtypeStruct(xc.shape, xc.dtype)],
        in_specs=[smem, smem, smem, vmem, vmem, pl.BlockSpec(memory_space=pl.ANY)],
        out_specs=[vmem, vmem],
        scratch_shapes=[
            VMEM((RING, CHUNK) + tiles.shape[1:], tiles.dtype),
            VMEM((17, k, n), jnp.float32),
            VMEM((9, k, n), jnp.float32),
            pltpu.SemaphoreType.DMA((RING,)),
        ],
        compiler_params=pltpu.CompilerParams(vmem_limit_bytes=40 << 20),
        name="products",
    )(count, rows, cols, xr, xc, tiles)


REDUCE_SENDS = 44


def add_into(dst, index, *others):
    total = dst[index].astype(jnp.float32)
    for ref, at in others:
        total += ref[at].astype(jnp.float32)
    dst[index] = total.astype(jnp.bfloat16)


def reduce_kernel(
    pr, pc, out, a, b, m_buf, x_half, x_buf, z_buf, y_half, y_buf, zf_buf,
    load, send_sems, m_in, fx_in, x_in, z_in, fy_in, y_in, zf_in,
):
    net = Net()
    send = Sends(send_sems)
    order = ((1, 1), (3, 1), (2, 1), (2, 0), (1, 0), (3, 0), (0, 1), (0, 0))
    loads = {}
    for n, (d, p) in enumerate(order):
        loads[d, p] = [
            pltpu.make_async_copy(pr.at[net.own_col(d, p)], a.at[d, p], load.at[0, n]),
            pltpu.make_async_copy(pc.at[net.own_row(d, p)], b.at[d, p], load.at[1, n]),
        ]
        for copy in loads[d, p]:
            copy.start()
    net.barrier()
    for d, p in order:
        for h in range(2):
            send(pr.at[net.mate_col(d, p), half(h)], m_buf.at[d, p, half(h)], m_in.at[d, p, h], net.mate)

    def from_mate(d, p, h):
        await_copy(m_buf.at[d, p, half(h)], m_in.at[d, p, h])
        add_into(a, (d, p, half(h)), (m_buf, (d, p, half(h))))

    x_peers, y_peers = (net.right, net.left), (net.up, net.down)
    dist = (1, 3)

    def x_send(way, p, h):
        d = dist[way]
        send(a.at[d, p, half(h)], x_buf.at[way, p, half(h)], x_in.at[way, p, h], x_peers[way])

    def y_send(way, q, h):
        d = dist[way]
        send(b.at[d, q, half(h)], y_buf.at[way, q, half(h)], y_in.at[way, q, h], y_peers[way])

    def y_far(way, q):
        send(b.at[2, q, half(way)], y_half.at[way, q], fy_in.at[way, q], y_peers[way])

    def y_join(way, q):
        await_copy(y_half.at[way, q], fy_in.at[way, q])
        add_into(b, (dist[way], q, half(way)), (y_half, (way, q)))
        y_send(way, q, way)

    loads[2, 1][1].wait()
    for way in range(2):
        y_far(way, 1)
    for way in range(2):
        loads[dist[way], 1][1].wait()
        y_send(way, 1, 1 - way)
    for way in range(2):
        loads[dist[way], 1][0].wait()
        for h in range(2):
            from_mate(dist[way], 1, h)
            x_send(way, 1, h)
    loads[2, 1][0].wait()
    for h in range(2):
        from_mate(2, 1, h)
        send(a.at[2, 1, half(h)], z_buf.at[1, half(h)], z_in.at[1, h], net.zpair)
    for way in range(2):
        y_join(way, 1)
    for way in range(2):
        loads[dist[way], 0][0].wait()
        from_mate(dist[way], 0, 1 - way)
        x_send(way, 0, 1 - way)
    loads[2, 0][1].wait()
    for way in range(2):
        y_far(way, 0)
    for way in range(2):
        loads[dist[way], 0][1].wait()
        y_send(way, 0, 1 - way)
    loads[2, 0][0].wait()
    for way in range(2):
        from_mate(2, 0, way)
        await_copy(z_buf.at[1, half(way)], z_in.at[1, way])
        add_into(a, (2, 0, half(way)), (z_buf, (1, half(way))))
        send(a.at[2, 0, half(way)], x_half.at[way], fx_in.at[way], x_peers[way])
    for way in range(2):
        from_mate(dist[way], 0, way)
    for p in (1, 0):
        loads[0, p][0].wait()
        loads[0, p][1].wait()
        for h in range(2):
            from_mate(0, p, h)

    def x_total(p, h):
        for way in range(2):
            await_copy(x_buf.at[way, p, half(h)], x_in.at[way, p, h])
        add_into(a, (0, p, half(h)), (x_buf, (0, p, half(h))), (x_buf, (1, p, half(h))))

    def y_total(q, h):
        for way in range(2):
            await_copy(y_buf.at[way, q, half(h)], y_in.at[way, q, h])
        add_into(b, (0, q, half(h)), (y_buf, (0, q, half(h))), (y_buf, (1, q, half(h))))

    for h in range(2):
        x_total(1, h)
        send(a.at[0, 1, half(h)], z_buf.at[0, half(h)], z_in.at[0, h], net.zpair)
    for h in range(2):
        y_total(1, h)
        send(b.at[0, 1, half(h)], zf_buf.at[half(h)], zf_in.at[h], net.zfar)
    for way in range(2):
        await_copy(x_half.at[way], fx_in.at[way])
        add_into(a, (dist[way], 0, half(way)), (x_half, (way,)))
        x_send(way, 0, way)
        y_join(way, 0)
    for h in range(2):
        x_total(0, h)
        y_total(0, h)
        await_copy(z_buf.at[0, half(h)], z_in.at[0, h])
        await_copy(zf_buf.at[half(h)], zf_in.at[h])
        total = a[0, 0, half(h)].astype(jnp.float32) + z_buf[0, half(h)].astype(jnp.float32)
        total += b[0, 0, half(h)].astype(jnp.float32)
        total += zf_buf[half(h)].astype(jnp.float32)
        out[half(h)] = total.astype(jnp.bfloat16)
    send.drain()
    assert len(send.copies) == REDUCE_SENDS, len(send.copies)


def reduce_scatter(pr, pc):
    k, n = pr.shape[1:]
    dma = pltpu.SemaphoreType.DMA
    blk = lambda *lead: VMEM((*lead, k, n), jnp.bfloat16)
    hlf = lambda *lead: VMEM((*lead, HALF, n), jnp.bfloat16)
    return pl.pallas_call(
        reduce_kernel,
        out_shape=jax.ShapeDtypeStruct((k, n), jnp.bfloat16),
        in_specs=[pl.BlockSpec(memory_space=pl.ANY)] * 2,
        out_specs=pl.BlockSpec(memory_space=VMEM),
        scratch_shapes=[
            blk(4, 2), blk(4, 2), blk(4, 2), hlf(2), blk(2, 2), blk(2), hlf(2, 2), blk(2, 2), blk(),
            dma((2, 8)), dma((REDUCE_SENDS,)), dma((4, 2, 2)), dma((2,)), dma((2, 2, 2)), dma((2, 2)),
            dma((2, 2)), dma((2, 2, 2)), dma((2,)),
        ],
        compiler_params=pltpu.CompilerParams(collective_id=1, has_side_effects=True, vmem_limit_bytes=16 << 20),
        name="panel_sums",
    )(pr, pc)


def shards(vectors, tile_values, tile_rows, tile_cols, tile_count):
    xr, xc = gather(vectors)
    pr, pc = products(tile_count, tile_rows, tile_cols, xr, xc, tile_values)
    return reduce_scatter(pr, pc)


def solution(mesh):
    in_specs = (
        P(None, ("row", "col")),
        P(("row", "col"), None, None),
        P(("row", "col")),
        P(("row", "col")),
        P(("row", "col")),
    )
    out_specs = P(None, ("row", "col"))
    return jax.shard_map(shards, mesh=mesh, in_specs=in_specs, out_specs=out_specs, check_vma=False)
```

profile of v0, /device:TPU:0, one launch (start us, length us, event | category | flops | bytes accessed | tf_op | source)
XLA Modules:
  0.0 73.8 jit_solution(12033082353854092965)
XLA Ops:
  0.7 0.0 copy-start
  0.7 0.9 %copy-done = bf16[32,4096]{1,0:T(8,128)(2,1)S(1)} copy-done((bf16[32,4096]{1,0:T(8,128)(2,1)S(1)}, bf16[32,4096]{1,0:T(8,128)(2,1)}, u32[]{:S(2)}) %copy-start) | copy-done | bytes 262168
  1.6 26.4 %panels.1 = (bf16[16,32,4096]{2,1,0:T(8,128)(2,1)S(1)}, bf16[8,32,4096]{2,1,0:T(8,128)(2,1)S(1)}) custom-call(bf16[32,4096]{1,0:T(8,128)(2,1)S(1)} %copy-done), custom_call_target="tpu_custom_call" | custom-call | tf_op jit(solution)/shard_map/panels/pallas_call | solution.py:190
  28.0 0.0 copy-start.1
  28.0 0.7 copy-done.1
  28.7 0.0 copy-start.2
  28.7 0.7 copy-done.2
  29.3 16.7 %products.1 = (bf16[16,32,4096]{2,1,0:T(8,128)(2,1)S(1)}, bf16[8,32,4096]{2,1,0:T(8,128)(2,1)S(1)}) custom-call(s32[1]{0:T(128)S(6)} %copy.7.count, s32[640]{0:T(1024)S(1)} %copy-done.1, s32[640]{0:T(1024)S(1)} %copy-done.2, bf16[16,32,4096]{2,1,0:T(8,128)(2,1)S(1)} %get-tuple-element.9.xr, bf16[8,32,4096]{2,1,0:T(8,128)(2,1)S(1)} %get-tuple-element.10.xc, ...), custom_call_target="tpu_custom_call" | custom-call | tf_op jit(solution)/shard_map/products/pallas_call | solution.py:284
  46.0 27.1 %panel_sums.1 = bf16[32,4096]{1,0:T(8,128)(2,1)S(1)} custom-call(bf16[16,32,4096]{2,1,0:T(8,128)(2,1)S(1)} %get-tuple-element.11.pr, bf16[8,32,4096]{2,1,0:T(8,128)(2,1)S(1)} %get-tuple-element.12.pc), custom_call_target="tpu_custom_call" | custom-call | tf_op jit(solution)/shard_map/panel_sums/pallas_call | solution.py:433
  73.1 0.7 copy.8
Async XLA Ops:
  0.7 1.0 %copy-start = (bf16[32,4096]{1,0:T(8,128)(2,1)S(1)}, bf16[32,4096]{1,0:T(8,128)(2,1)}, u32[]{:S(2)}) copy-start(bf16[32,4096]{1,0:T(8,128)(2,1)} %v.1) | copy-start | bytes 786436
  28.0 0.7 copy-start.1
  28.7 0.7 copy-start.2
where the time goes:
time: 75.1 us; the launch traced here: 73.8 us
  Pallas kernels  70.1 us (93%)
  local copies, waits for them, and re-layouts  3.02 us (4%)
    pallas_call x1, Pallas kernels, reduce_scatter(): pl.pallas_call(reduce_kernel, out_shape=jax.ShapeDtypeStruct((k, n), jnp....  27.1 us
    pallas_call x1, Pallas kernels, gather(): pl.pallas_call(gather_kernel, out_shape=[jax.ShapeDtypeStruct((16, k, n),...  26.4 us
    pallas_call x1, Pallas kernels, products(): pl.pallas_call(product_kernel, out_shape=[jax.ShapeDtypeStruct(xr.shape,...  16.7 us
    unnamed x7, local copies, waits for them, and re-layouts  3.02 us

commit v1 on v0

--- a/solution.py
+++ b/solution.py
@@ -10,7 +10,7 @@
 HALF = 16
 CHUNK = 32
 UNROLL = 16
-RING = 8
+GROUPS = CHUNK // UNROLL
 
 
 def place():
@@ -86,9 +86,11 @@
 
 
 GATHER_SENDS = 44
-
-
-def gather_kernel(v, xr, xc, keep, send_sems, z_in, x_in, fx_in, m_in, zf_in, y_in, fy_in):
+TILE_COPIES = 4
+VMEM_GRANT = 18 << 20
+
+
+def gather_kernel(v, rows_hbm, cols_hbm, tiles_hbm, xr, xc, rows, cols, tiles, keep, send_sems, z_in, x_in, fx_in, m_in, zf_in, y_in, fy_in):
     net = Net()
     send = Sends(send_sems)
 
@@ -104,7 +106,12 @@
     own = [
         pltpu.make_async_copy(v, xr.at[net.col], keep.at[0]),
         pltpu.make_async_copy(v, xc.at[net.row], keep.at[1]),
+        pltpu.make_async_copy(rows_hbm, rows, keep.at[2]),
+        pltpu.make_async_copy(cols_hbm, cols, keep.at[3]),
     ]
+    for i in range(TILE_COPIES):
+        part = pl.ds(i * (tiles.shape[0] // TILE_COPIES), tiles.shape[0] // TILE_COPIES)
+        own.append(pltpu.make_async_copy(tiles_hbm.at[part], tiles.at[part], keep.at[4 + i]))
     net.barrier()
     for h in range(2):
         send(v.at[half(h)], c_at(0, 0, h), zf_in.at[h], net.zfar)
@@ -184,16 +191,17 @@
     assert len(send.copies) == GATHER_SENDS
 
 
-def gather(v):
+def gather(v, rows, cols, tiles):
     k, n = v.shape
     dma = pltpu.SemaphoreType.DMA
     return pl.pallas_call(
         gather_kernel,
-        out_shape=[jax.ShapeDtypeStruct((16, k, n), v.dtype), jax.ShapeDtypeStruct((8, k, n), v.dtype)],
-        in_specs=[pl.BlockSpec(memory_space=VMEM)],
-        out_specs=[pl.BlockSpec(memory_space=pl.ANY)] * 2,
+        out_shape=[jax.ShapeDtypeStruct((16, k, n), v.dtype), jax.ShapeDtypeStruct((8, k, n), v.dtype)]
+        + [jax.ShapeDtypeStruct(a.shape, a.dtype) for a in (rows, cols, tiles)],
+        in_specs=[pl.BlockSpec(memory_space=pltpu.HBM)] * 4,
+        out_specs=[pl.BlockSpec(memory_space=pl.ANY)] * 5,
         scratch_shapes=[
-            dma((2,)),
+            dma((4 + TILE_COPIES,)),
             dma((GATHER_SENDS,)),
             dma((2, 2)),
             dma((2, 2, 2)),
@@ -203,22 +211,21 @@
             dma((2, 2, 2)),
             dma((2, 2)),
         ],
-        compiler_params=pltpu.CompilerParams(collective_id=0, has_side_effects=True, vmem_limit_bytes=4 << 20),
+        compiler_params=pltpu.CompilerParams(collective_id=0, has_side_effects=True, vmem_limit_bytes=VMEM_GRANT),
         name="panels",
-    )(v)
-
-
-def product_kernel(count, rows, cols, xr, xc, tiles_hbm, out_r, out_c, tiles, acc_r, acc_c, sems):
+    )(v, rows, cols, tiles)
+
+
+def product_kernel(count, rows_hbm, cols_hbm, xr, xc, tiles, out_r, out_c, rows, cols, acc_r, acc_c,
+                   stage_r0, stage_c0, stage_r1, stage_c1, sems):
+    lists = [
+        pltpu.make_async_copy(rows_hbm, rows, sems.at[0]),
+        pltpu.make_async_copy(cols_hbm, cols, sems.at[1]),
+    ]
+    for copy in lists:
+        copy.start()
     live = count[0]
     chunks = (live + CHUNK - 1) // CHUNK
-
-    def fetch(i):
-        n = lax.rem(i, RING)
-        return pltpu.make_async_copy(tiles_hbm.at[pl.ds(i * CHUNK, CHUNK)], tiles.at[n], sems.at[n])
-
-    @pl.loop(0, jnp.minimum(chunks, RING))
-    def _(i):
-        fetch(i).start()
 
     @pl.loop(0, 16)
     def _(i):
@@ -228,45 +235,50 @@
     def _(i):
         acc_c[i] = jnp.zeros(acc_c.shape[1:], jnp.float32)
 
+    for copy in lists:
+        copy.wait()
+
     def lanes(block):
-        return pl.ds(pl.multiple_of(lax.rem(block, 32) * 128, 128), 128)
+        return pl.ds(pl.multiple_of((block & 31) * 128, 128), 128)
 
     none = jnp.zeros((32, 128), jnp.bfloat16)
 
     def both(x, y):
         return jnp.concatenate([jnp.concatenate([x, none], axis=1), jnp.concatenate([none, y], axis=1)], axis=0)
 
+    def multiply(s, u, stage_r, stage_c):
+        rb, cb = [rows[s], rows[s + 1]], [cols[s], cols[s + 1]]
+        t = tiles[pl.ds(s, 2)]
+        x_c = both(*[xc[b >> 5, :, lanes(b)] for b in cb])
+        x_r = both(*[xr[b >> 5, :, lanes(b)] for b in rb])
+        flip = jnp.concatenate([t[0].T, t[1].T], axis=0)
+        to_r = lax.dot_general(x_c, flip, (((1,), (0,)), ((), ())), preferred_element_type=jnp.float32)
+        tall = t.reshape(256, 128)
+        to_c = lax.dot_general(x_r, tall, (((1,), (0,)), ((), ())), preferred_element_type=jnp.float32)
+        stage_r[pl.ds(32 * u, 64)] = to_r
+        stage_c[pl.ds(32 * u, 64)] = to_c
+
+    def add_up(g, u, stage_r, stage_c):
+        s = jnp.maximum(g, 0) * UNROLL + u
+        ok = (g >= 0) & (s < live)
+        rb, cb = rows[s], cols[s]
+        rd = jnp.where(ok, rb >> 5, 16)
+        cd = jnp.where(ok, cb >> 5, 8)
+        acc_r[rd, :, lanes(rb)] += stage_r[pl.ds(32 * u, 32)]
+        acc_c[cd, :, lanes(cb)] += stage_c[pl.ds(32 * u, 32)]
+
+    stages = ((stage_r0, stage_c0), (stage_r1, stage_c1))
+
     @pl.loop(0, chunks)
     def _(i):
-        fetch(i).wait()
-        n = lax.rem(i, RING)
-
-        @pl.loop(0, CHUNK // UNROLL)
-        def _(j):
-            found = []
+        for part in range(GROUPS):
             for u in range(0, UNROLL, 2):
-                at = j * UNROLL + u
-                s = i * CHUNK + at
-                rb, cb = [rows[s], rows[s + 1]], [cols[s], cols[s + 1]]
-                t = tiles[n, pl.ds(at, 2)]
-                x_c = both(*[xc[b // 32, :, lanes(b)] for b in cb])
-                x_r = both(*[xr[b // 32, :, lanes(b)] for b in rb])
-                wide = jnp.concatenate([t[0], t[1]], axis=1)
-                to_r = lax.dot_general(x_c, wide, (((1,), (1,)), ((), ())), preferred_element_type=jnp.float32)
-                tall = t.reshape(256, 128)
-                to_c = lax.dot_general(x_r, tall, (((1,), (0,)), ((), ())), preferred_element_type=jnp.float32)
+                multiply(i * CHUNK + part * UNROLL + u, u, *stages[part % 2])
                 for e in range(2):
-                    part = slice(32 * e, 32 * e + 32)
-                    found.append((rb[e], cb[e], s + e < live, to_r[part], to_c[part]))
-            for rb, cb, ok, to_r, to_c in found:
-                rd = jnp.where(ok, rb // 32, 16)
-                cd = jnp.where(ok, cb // 32, 8)
-                acc_r[rd, :, lanes(rb)] += to_r
-                acc_c[cd, :, lanes(cb)] += to_c
-
-        @pl.when(i + RING < chunks)
-        def _():
-            fetch(i + RING).start()
+                    add_up(i * GROUPS + part - 1, u + e, *stages[1 - part % 2])
+
+    for u in range(UNROLL):
+        add_up(chunks * GROUPS - 1, u, *stages[(GROUPS - 1) % 2])
 
     @pl.loop(0, 16)
     def _(i):
@@ -281,18 +293,21 @@
     k, n = xr.shape[1:]
     smem = pl.BlockSpec(memory_space=pltpu.SMEM)
     vmem = pl.BlockSpec(memory_space=VMEM)
+    keep = pl.BlockSpec(memory_space=pl.ANY)
     return pl.pallas_call(
         product_kernel,
         out_shape=[jax.ShapeDtypeStruct(xr.shape, xr.dtype), jax.ShapeDtypeStruct(xc.shape, xc.dtype)],
-        in_specs=[smem, smem, smem, vmem, vmem, pl.BlockSpec(memory_space=pl.ANY)],
+        in_specs=[smem, keep, keep, vmem, vmem, vmem],
         out_specs=[vmem, vmem],
         scratch_shapes=[
-            VMEM((RING, CHUNK) + tiles.shape[1:], tiles.dtype),
+            pltpu.SMEM(rows.shape, rows.dtype),
+            pltpu.SMEM(cols.shape, cols.dtype),
             VMEM((17, k, n), jnp.float32),
             VMEM((9, k, n), jnp.float32),
-            pltpu.SemaphoreType.DMA((RING,)),
+            *[VMEM((32 * UNROLL, 128), jnp.float32)] * 4,
+            pltpu.SemaphoreType.DMA((2,)),
         ],
-        compiler_params=pltpu.CompilerParams(vmem_limit_bytes=40 << 20),
+        compiler_params=pltpu.CompilerParams(vmem_limit_bytes=VMEM_GRANT),
         name="products",
     )(count, rows, cols, xr, xc, tiles)
 
@@ -446,8 +461,9 @@
 
 
 def shards(vectors, tile_values, tile_rows, tile_cols, tile_count):
-    xr, xc = gather(vectors)
-    pr, pc = products(tile_count, tile_rows, tile_cols, xr, xc, tile_values)
+    held = [pltpu.with_memory_space_constraint(a, pltpu.HBM) for a in (vectors, tile_rows, tile_cols, tile_values)]
+    xr, xc, rows, cols, tiles = gather(*held)
+    pr, pc = products(tile_count, rows, cols, xr, xc, tiles)
     return reduce_scatter(pr, pc)
 
 

time: 75.1 us -> 69.2 us (0.921)
  Pallas kernels: 70.1 us -> 67 us
  local copies, waits for them, and re-layouts: 3.02 us -> 0.71 us
    pallas_call x1, Pallas kernels: 16.7 us -> 7.46 us  [products(): pl.pallas_call(product_kernel, out_shape=[jax.ShapeDtypeStruct(xr.shape,...]
    pallas_call x1, Pallas kernels: 27.1 us -> 32.7 us  [reduce_scatter(): pl.pallas_call(reduce_kernel, out_shape=jax.ShapeDtypeStruct((k, n), jnp....]
    unnamed x7 -> x1, local copies, waits for them, and re-layouts: 3.02 us -> 0.71 us
where the time goes in v1:
time: 69.2 us; the launch traced here: 68.4 us
  Pallas kernels  67 us (97%)
  local copies, waits for them, and re-layouts  0.71 us (1%)
    pallas_call x1, Pallas kernels, reduce_scatter(): pl.pallas_call(reduce_kernel, out_shape=jax.ShapeDtypeStruct((k, n), jnp....  32.7 us
    pallas_call x1, Pallas kernels, gather(): pl.pallas_call(gather_kernel, out_shape=[jax.ShapeDtypeStruct((16, k, n),...  26.8 us
    pallas_call x1, Pallas kernels, products(): pl.pallas_call(product_kernel, out_shape=[jax.ShapeDtypeStruct(xr.shape,...  7.46 us

profile of v1, /device:TPU:0, one launch (start us, length us, event | category | flops | bytes accessed | tf_op | source)
XLA Modules:
  0.0 68.4 jit_solution(7164200042174159888)
XLA Ops:
  0.7 26.8 %panels.1 = (bf16[16,32,4096]{2,1,0:T(8,128)(2,1)S(1)}, bf16[8,32,4096]{2,1,0:T(8,128)(2,1)S(1)}, s32[640]{0:T(1024)S(1)}, s32[640]{0:T(1024)S(1)}, bf16[640,128,128]{2,1,0:T(8,128)(2,1)S(1)}) custom-call(bf16[32,4096]{1,0:T(8,128)(2,1)} %v.1, s32[640]{0:T(1024)} %rows_hbm.1, s32[640]{0:T(1024)} %cols_hbm.1, bf16[640,128,128]{2,1,0:T(8,128)(2,1)} %tiles_hbm.1), custom_call_target="tpu_custom_call" | custom-call | tf_op jit(solution)/shard_map/panels/pallas_call | solution.py:197
  27.5 7.5 %products.1 = (bf16[16,32,4096]{2,1,0:T(8,128)(2,1)S(1)}, bf16[8,32,4096]{2,1,0:T(8,128)(2,1)S(1)}) custom-call(s32[1]{0:T(128)S(6)} %copy.7.count, s32[640]{0:T(1024)S(1)} %get-tuple-element.12.rows_hbm, s32[640]{0:T(1024)S(1)} %get-tuple-element.13.cols_hbm, bf16[16,32,4096]{2,1,0:T(8,128)(2,1)S(1)} %get-tuple-element.14.xr, ...), custom_call_target="tpu_custom_call" | custom-call | tf_op jit(solution)/shard_map/products/pallas_call | solution.py:297
  35.0 32.7 %panel_sums.1 = bf16[32,4096]{1,0:T(8,128)(2,1)S(1)} custom-call(bf16[16,32,4096]{2,1,0:T(8,128)(2,1)S(1)} %get-tuple-element.17.pr, bf16[8,32,4096]{2,1,0:T(8,128)(2,1)S(1)} %get-tuple-element.18.pc), custom_call_target="tpu_custom_call" | custom-call | tf_op jit(solution)/shard_map/panel_sums/pallas_call | solution.py:448
  67.7 0.7 %copy.8 = bf16[32,4096]{1,0:T(8,128)(2,1)} copy(bf16[32,4096]{1,0:T(8,128)(2,1)S(1)} %panel_sums.1) | data formatting | bytes 524288
